TPU v7x, 32 devices: a whole 2x2x4 slice. The times are simulated.
32 devices in a mesh: comp: 2 (over core), gy: 4 (over y, x), gx: 4 (over z).
Axes of the slice: x: 2, y: 2, z: 4, core: 2. Of those that a mesh axis runs over, the one named last changes fastest.
Arguments:
- ocean_state: float32 [16, 8, 16, 512], P('comp', None, 'gx', 'gy'), may hold values from -4 to 4, as said below
- irradiance: float32 [16, 512], P('gx', 'gy'), may hold values from 0.5 to 4
- land_mask: int32 [16, 512], P('gx', 'gy'), may hold values 0 or 1
- bottom_level: int32 [16, 512], P('gx', 'gy'), may hold values from 1 to 8
Outputs:
- new_state: float32 [16, 8, 16, 512], P('comp', None, 'gx', 'gy')
Inputs may be any that keep to these rules, and one draw needn't show every extreme that they name: `ocean_state`: channels 0 to 3 hold velocity along x, velocity along y, temperature and salinity now, channels 4 to 7 the same one step earlier; the 8 tracer channels are positive.
All inputs are finite; a program needn't handle non-finite values. No bound on the sum of `land_mask` on one device may be relied on, other than what follows from the above.
Results may differ from a plain program's by a relative error of at most 0.0003.
Values sent between devices are 32-bit elements; how exact they have to be, the bound alone decides.
No kernel may reach another device: no remote copies, remote signals or barrier semaphores. Data moves between devices by JAX's collectives and lax.ppermute only.
A program may use at most 64 MiB of HBM per device.

v0:
```python
import jax
import jax.numpy as jnp
from jax import lax
from jax.sharding import PartitionSpec as P

STEPS = 2
TIME_STEP = 0.1
VISCOSITY = 0.2
DIFFUSION = 0.2
ASSELIN_GAIN = 0.1
THERMAL_EXPAND = 0.2
HALINE_CONTRACT = 0.8
GRAVITY_STEP = 0.1
CORIOLIS_BASE = 0.3
CORIOLIS_SLOPE = 0.4
MIXING_FLOOR = 0.05
MIXING_SPAN = 1.0
STRATIFICATION = 4.0
HEATING_GAIN = 3.0
WATER_ABSORB = 0.08
PIGMENT_ABSORB = 0.05
LIGHT_HALF = 0.5
THERMAL_GAIN_PER = 0.06
GROWTH_SMALL = 0.6
GROWTH_LARGE = 0.9
NUTRIENT_HALF_SMALL = 0.2
NUTRIENT_HALF_LARGE = 0.8
GRAZING_RATE = 0.8
GRAZING_HALF = 1.0
PHYTO_DEATH = 0.1
ZOOPLANKTON_DEATH = 0.15
EXCRETION = 0.1
ASSIMILATION = 0.7
REMINERAL_SMALL = 0.3
REMINERAL_LARGE = 0.1
NITRIFICATION = 0.2
OXYGEN_YIELD = 1.3
OXYGEN_DEMAND = 1.0


def extended(shard, sides, width, wrap):
    for axis, dim in sides:
        count, length = (lax.axis_size(axis), shard.shape[dim])
        up = [(i, (i + 1) % count) for i in range(count if wrap else count - 1)]
        down = [(j, i) for i, j in up]
        last = lax.slice_in_dim(shard, length - width, length, axis=dim)
        leading = lax.slice_in_dim(shard, 0, width, axis=dim)
        before = lax.ppermute(last, axis, up)
        after = lax.ppermute(leading, axis, down)
        shard = jnp.concatenate([before, shard, after], axis=dim)
    return shard


def broadcast(shard, axis, root):
    mine = lax.axis_index(axis) == root
    return lax.psum(jnp.where(mine, shard, jnp.zeros_like(shard)), axis)


def interior(field_in):
    return field_in[..., 1:-1, 1:-1]


def neighbours(field_in):
    return (
        field_in[..., 2:, 1:-1],
        field_in[..., :-2, 1:-1],
        field_in[..., 1:-1, 2:],
        field_in[..., 1:-1, :-2],
    )


def laplacian(field_in, entire_ocean_indicator):
    centre = interior(field_in)
    total = jnp.zeros_like(centre)
    for other, wet_other in zip(neighbours(field_in), neighbours(entire_ocean_indicator)):
        total = total + wet_other * (other - centre)
    return total * interior(entire_ocean_indicator)


def advection(east_speed, north_speed, field_in, entire_ocean_indicator):
    centre = interior(field_in)
    wet_centre = interior(entire_ocean_indicator)
    east_centre = interior(east_speed)
    north_centre = interior(north_speed)
    field_near = neighbours(field_in)
    wet_near = neighbours(entire_ocean_indicator)
    east_near = neighbours(east_speed)
    north_near = neighbours(north_speed)
    flux_east = (
        0.25 * (east_centre + east_near[0]) * (centre + field_near[0]) * wet_centre * wet_near[0]
    )
    flux_west = (
        0.25 * (east_centre + east_near[1]) * (centre + field_near[1]) * wet_centre * wet_near[1]
    )
    flux_north = (
        0.25 * (north_centre + north_near[2]) * (centre + field_near[2]) * wet_centre * wet_near[2]
    )
    flux_south = (
        0.25 * (north_centre + north_near[3]) * (centre + field_near[3]) * wet_centre * wet_near[3]
    )
    return flux_east - flux_west + flux_north - flux_south


def pressure_force(pressure, entire_ocean_indicator):
    centre = interior(pressure)
    wet_centre = interior(entire_ocean_indicator)
    near = neighbours(pressure)
    wet_near = neighbours(entire_ocean_indicator)
    force_east = (
        0.5 * wet_centre * (wet_near[0] * (near[0] - centre) + wet_near[1] * (centre - near[1]))
    )
    force_north = (
        0.5 * wet_centre * (wet_near[2] * (near[2] - centre) + wet_near[3] * (centre - near[3]))
    )
    return (force_east, force_north)


def ocean_water_mass_per_volume(thermal_state_grid, salt_content_grid, entire_ocean_indicator):
    return (
        HALINE_CONTRACT * salt_content_grid - THERMAL_EXPAND * thermal_state_grid
    ) * entire_ocean_indicator


def make_flow(dynamics_full, entire_ocean_indicator):
    density = ocean_water_mass_per_volume(
        dynamics_full[2], dynamics_full[3], entire_ocean_indicator
    )
    below = jnp.concatenate([density[1:], density[-1:]], axis=0)
    wet_below = jnp.concatenate(
        [entire_ocean_indicator[1:], jnp.zeros_like(entire_ocean_indicator[:1])], axis=0
    )
    strat = jnp.maximum(below - density, 0.0)
    mixing = (
        (MIXING_FLOOR + MIXING_SPAN / (1.0 + STRATIFICATION * strat))
        * entire_ocean_indicator
        * wet_below
    )
    return jnp.stack([dynamics_full[0], dynamics_full[1], dynamics_full[2], mixing], axis=0)


def absorption(arriving_constituents, lit_in):
    wet_centre = (lit_in > 0).astype(jnp.float32)
    surface = lit_in[0]
    pigment = jnp.abs(arriving_constituents[2]) + jnp.abs(arriving_constituents[3])
    absorb = WATER_ABSORB + PIGMENT_ABSORB * pigment
    column = jnp.cumsum(absorb, axis=0)
    heating = surface * (jnp.exp(absorb - column) - jnp.exp(-column)) * wet_centre
    middle = surface * jnp.exp(0.5 * absorb - column)
    return (heating, middle)


def biotic_source_terms(arriving_constituents, thermal_state_grid, layer_centre_irradiance):
    nitrate, ammonium, small_phyto, large_phyto = (
        arriving_constituents[0],
        arriving_constituents[1],
        arriving_constituents[2],
        arriving_constituents[3],
    )
    grazers, small_detritus, large_detritus = (
        arriving_constituents[4],
        arriving_constituents[5],
        arriving_constituents[6],
    )
    nitrate_size = jnp.abs(nitrate)
    ammonium_size = jnp.abs(ammonium)
    light_limit = layer_centre_irradiance / (layer_centre_irradiance + LIGHT_HALF)
    thermal_change_per_step = jnp.exp(THERMAL_GAIN_PER * thermal_state_grid)
    small_common = (
        GROWTH_SMALL
        * thermal_change_per_step
        * light_limit
        * small_phyto
        / (NUTRIENT_HALF_SMALL + nitrate_size + ammonium_size)
    )
    large_common = (
        GROWTH_LARGE
        * thermal_change_per_step
        * light_limit
        * large_phyto
        / (NUTRIENT_HALF_LARGE + nitrate_size + ammonium_size)
    )
    small_nitrate = small_common * nitrate_size
    small_ammonium = small_common * ammonium_size
    large_nitrate = large_common * nitrate_size
    large_ammonium = large_common * ammonium_size
    prey = jnp.abs(small_phyto) + jnp.abs(large_phyto)
    graze_factor = GRAZING_RATE * grazers / (GRAZING_HALF + prey)
    graze_small = graze_factor * small_phyto
    graze_large = graze_factor * large_phyto
    remin = REMINERAL_SMALL * small_detritus + REMINERAL_LARGE * large_detritus
    nitrify = NITRIFICATION * ammonium
    growth = small_nitrate + small_ammonium + large_nitrate + large_ammonium
    tend_nitrate = nitrify - small_nitrate - large_nitrate
    tend_ammonium = remin + EXCRETION * grazers - nitrify - small_ammonium - large_ammonium
    tend_small = small_nitrate + small_ammonium - graze_small - PHYTO_DEATH * small_phyto
    tend_large = large_nitrate + large_ammonium - graze_large - PHYTO_DEATH * large_phyto
    tend_grazers = (
        ASSIMILATION * (graze_small + graze_large)
        - EXCRETION * grazers
        - ZOOPLANKTON_DEATH * grazers
    )
    tend_small_det = (
        PHYTO_DEATH * small_phyto
        + (1.0 - ASSIMILATION) * graze_small
        - REMINERAL_SMALL * small_detritus
    )
    tend_large_det = (
        PHYTO_DEATH * large_phyto
        + ZOOPLANKTON_DEATH * grazers
        + (1.0 - ASSIMILATION) * graze_large
        - REMINERAL_LARGE * large_detritus
    )
    tend_oxygen = OXYGEN_YIELD * growth - OXYGEN_DEMAND * (remin + 2.0 * nitrify)
    return jnp.stack(
        [
            tend_nitrate,
            tend_ammonium,
            tend_small,
            tend_large,
            tend_grazers,
            tend_small_det,
            tend_large_det,
            tend_oxygen,
        ],
        axis=0,
    )


def dynamics_update(dynamics_full, entire_ocean_indicator, heating, row_start, total_rows):
    wet_centre = interior(entire_ocean_indicator)
    density = ocean_water_mass_per_volume(
        dynamics_full[2], dynamics_full[3], entire_ocean_indicator
    )
    pressure = GRAVITY_STEP * jnp.cumsum(density, axis=0)
    force_east, force_north = pressure_force(pressure, entire_ocean_indicator)
    row_count = dynamics_full.shape[3] - 2
    row_index = (jnp.arange(row_count, dtype=jnp.int32) + row_start + 1).astype(jnp.float32)
    coriolis = CORIOLIS_BASE + CORIOLIS_SLOPE * row_index / total_rows
    earlier = dynamics_full[4:8]
    diffused = laplacian(earlier, entire_ocean_indicator)
    carried = advection(
        dynamics_full[0], dynamics_full[1], dynamics_full[2:4], entire_ocean_indicator
    )
    now_centre = interior(dynamics_full[0:4])
    tend_east = coriolis * now_centre[1] - force_east + VISCOSITY * diffused[0]
    tend_north = -coriolis * now_centre[0] - force_north + VISCOSITY * diffused[1]
    tend_temp = -carried[0] + DIFFUSION * diffused[2] + HEATING_GAIN * heating
    tend_salt = -carried[1] + DIFFUSION * diffused[3]
    tendency = jnp.stack([tend_east, tend_north, tend_temp, tend_salt], axis=0)
    earlier_centre = interior(earlier)
    after = earlier_centre + 2.0 * TIME_STEP * tendency * wet_centre
    filtered = now_centre + ASSELIN_GAIN * (earlier_centre - 2.0 * now_centre + after) * wet_centre
    return jnp.concatenate([after, filtered], axis=0)


def tracer_update(tracers_full, flow_full, entire_ocean_indicator, middle):
    wet_centre = interior(entire_ocean_indicator)
    centre = interior(tracers_full)
    carried = advection(flow_full[0], flow_full[1], tracers_full, entire_ocean_indicator)
    spread = laplacian(tracers_full, entire_ocean_indicator)
    mixing = interior(flow_full[3])
    below = jnp.concatenate([centre[:, 1:], jnp.zeros_like(centre[:, :1])], axis=1)
    flux_down = mixing * (below - centre)
    flux_above = jnp.concatenate([jnp.zeros_like(flux_down[:, :1]), flux_down[:, :-1]], axis=1)
    vertical = flux_down - flux_above
    react = biotic_source_terms(centre, interior(flow_full[2]), middle)
    return centre + TIME_STEP * (DIFFUSION * spread - carried + vertical + react) * wet_centre


def extend(combined, width):
    widened = extended(combined, (("gx", 2),), width, True)
    result = extended(widened, (("gy", 3),), width, False)
    return result


def advance(padded, is_dynamics, row_start, total_rows):
    fields = padded[:-1]
    lit_full = padded[-1]
    entire_ocean_indicator = (lit_full > 0).astype(jnp.float32)

    def flow_source(fields_in, wet_in):
        return make_flow(fields_in, wet_in)

    def flow_empty(fields_in, wet_in):
        return jnp.zeros((4,) + wet_in.shape, jnp.float32)

    flow_out = lax.cond(is_dynamics, flow_source, flow_empty, fields, entire_ocean_indicator)

    def light_empty(fields_in, lit_in):
        blank = jnp.zeros(interior(lit_in).shape, jnp.float32)
        return (blank, blank)

    def light_source(fields_in, lit_in):
        return absorption(interior(fields_in), interior(lit_in))

    heat_out, middle = lax.cond(is_dynamics, light_empty, light_source, fields, lit_full)
    partner_flow = broadcast(flow_out, "comp", 0)
    heating = broadcast(heat_out, "comp", 1)

    def run_dynamics(fields_in, flow_in, heat_in, middle_in):
        return dynamics_update(fields_in, entire_ocean_indicator, heat_in, row_start, total_rows)

    def run_tracers(fields_in, flow_in, heat_in, middle_in):
        return tracer_update(fields_in, flow_in, entire_ocean_indicator, middle_in)

    return lax.cond(is_dynamics, run_dynamics, run_tracers, fields, partner_flow, heating, middle)


def local(ocean_state, irradiance, land_mask, bottom_level):
    depth_index = jnp.arange(ocean_state.shape[1], dtype=jnp.int32)[:, None, None]
    wet_cells = ((land_mask[None] == 1) & (depth_index < bottom_level[None])).astype(jnp.float32)
    lit_wet = irradiance[None] * wet_cells
    is_dynamics = lax.axis_index("comp") == 0
    local_rows = ocean_state.shape[3]
    total_rows = local_rows * lax.axis_size("gy")
    own_first_row = lax.axis_index("gy") * local_rows
    current = ocean_state
    padded = extend(jnp.concatenate([current, lit_wet[None]], axis=0), STEPS)
    for step_index in range(STEPS):
        margin = STEPS - step_index
        current = advance(padded, is_dynamics, own_first_row - margin, total_rows)
        padded = jnp.concatenate([current, interior(padded[-1:])], axis=0)
    return current


def solution(mesh):
    return jax.shard_map(
        local,
        mesh=mesh,
        in_specs=(P("comp", None, "gx", "gy"), P("gx", "gy"), P("gx", "gy"), P("gx", "gy")),
        out_specs=P("comp", None, "gx", "gy"),
        check_vma=False,
    )
```

profile of v0, /device:TPU:1, one launch (start us, length us, event | category | flops | bytes accessed | tf_op | source)
XLA Modules:
  0.0 91.3 jit_solution(18377207077706477353)
XLA Ops:
  6.5 0.7 broadcast_compare_fusion
  7.2 0.7 fusion.144
  7.9 1.1 %fusion.142 = (f32[9,8,2,128]{3,2,1,0:T(2,128)S(1)}, f32[9,8,2,128]{3,2,1,0:T(2,128)S(1)}) fusion(f32[8,8,4,128]{3,2,1,0:T(4,128)} %param.16, f32[1,8,4,128]{3,2,1,0:T(4,128)S(1)} %fusion.144), kind=kLoop, calls=%fused_computation.314 | loop fusion | flops 36864 | bytes 294912 | tf_op jit(solution)/shard_map/concatenate | solution.py:318
  9.1 2.2 %collective-permute-start = (f32[9,8,2,128]{3,2,1,0:T(2,128)S(1)}, f32[9,8,2,128]{3,2,1,0:T(2,128)S(1)}, u32[]{:S(2)}, u32[]{:S(2)}) collective-permute-start(f32[9,8,2,128]{3,2,1,0:T(2,128)S(1)} %get-tuple-element.212), channel_id=1, source_target_pairs={{0,1},{1,2},{2,3},{3,0},{4,5},{5,6},{6,7},{7,4},{8,9},{9,10},{10,1... | collective-permute-start | bytes 221192 | tf_op jit(solution)/shard_map/ppermute | solution.py:48
  11.2 2.1 %collective-permute-start.1 = (f32[9,8,2,128]{3,2,1,0:T(2,128)S(1)}, f32[9,8,2,128]{3,2,1,0:T(2,128)S(1)}, u32[]{:S(2)}, u32[]{:S(2)}) collective-permute-start(f32[9,8,2,128]{3,2,1,0:T(2,128)S(1)} %get-tuple-element.213), channel_id=1, source_target_pairs={{1,0},{2,1},{3,2},{0,3},{5,4},{6,5},{7,6},{4,7},{9,8},{10,9},{11,1... | collective-permute-start | bytes 221192 | tf_op jit(solution)/shard_map/ppermute | solution.py:49
  13.3 1.8 %collective-permute-done = f32[9,8,2,128]{3,2,1,0:T(2,128)S(1)} collective-permute-done((f32[9,8,2,128]{3,2,1,0:T(2,128)S(1)}, f32[9,8,2,128]{3,2,1,0:T(2,128)S(1)}, u32[]{:S(2)}, u32[]{:S(2)}) %collective-permute-start) | collective-permute-done | bytes 73760 | tf_op jit(solution)/shard_map/ppermute | solution.py:48
  15.1 1.3 %collective-permute-done.1 = f32[9,8,2,128]{3,2,1,0:T(2,128)S(1)} collective-permute-done((f32[9,8,2,128]{3,2,1,0:T(2,128)S(1)}, f32[9,8,2,128]{3,2,1,0:T(2,128)S(1)}, u32[]{:S(2)}, u32[]{:S(2)}) %collective-permute-start.1) | collective-permute-done | bytes 73760 | tf_op jit(solution)/shard_map/ppermute | solution.py:49
  16.7 2.8 %collective-permute-start.2 = (f32[9,8,8,2]{3,2,1,0:T(8,128)S(1)}, f32[9,8,8,2]{3,2,1,0:T(8,128)S(1)}, u32[]{:S(2)}, u32[]{:S(2)}) collective-permute-start(f32[9,8,8,2]{3,2,1,0:T(8,128)S(1)} %get-tuple-element.210), channel_id=1, source_target_pairs={{0,4},{4,8},{8,12},{1,5},{5,9},{9,13},{2,6},{6,10},{10,14},{3,7},{... | collective-permute-start | bytes 13832 | tf_op jit(solution)/shard_map/ppermute | solution.py:48
  19.5 1.3 %collective-permute-start.3 = (f32[9,8,8,2]{3,2,1,0:T(8,128)S(1)}, f32[9,8,8,2]{3,2,1,0:T(8,128)S(1)}, u32[]{:S(2)}, u32[]{:S(2)}) collective-permute-start(f32[9,8,8,2]{3,2,1,0:T(8,128)S(1)} %get-tuple-element.211), channel_id=1, source_target_pairs={{4,0},{8,4},{12,8},{5,1},{9,5},{13,9},{6,2},{10,6},{14,10},{7,3},{... | collective-permute-start | bytes 13832 | tf_op jit(solution)/shard_map/ppermute | solution.py:49
  20.8 3.6 %collective-permute-done.2 = f32[9,8,8,2]{3,2,1,0:T(8,128)S(1)} collective-permute-done((f32[9,8,8,2]{3,2,1,0:T(8,128)S(1)}, f32[9,8,8,2]{3,2,1,0:T(8,128)S(1)}, u32[]{:S(2)}, u32[]{:S(2)}) %collective-permute-start.2) | collective-permute-done | bytes 4640 | tf_op jit(solution)/shard_map/ppermute | solution.py:48
  24.4 8.3 %collective-permute-done.3 = f32[9,8,8,2]{3,2,1,0:T(8,128)S(1)} collective-permute-done((f32[9,8,8,2]{3,2,1,0:T(8,128)S(1)}, f32[9,8,8,2]{3,2,1,0:T(8,128)S(1)}, u32[]{:S(2)}, u32[]{:S(2)}) %collective-permute-start.3) | collective-permute-done | bytes 4640 | tf_op jit(solution)/shard_map/ppermute | solution.py:49
  33.5 0.7 broadcast_select_fusion.1
  34.6 5.6 %psum.29 = f32[8,6,130]{2,1,0:T(8,128)S(1)} all-reduce(f32[8,6,130]{2,1,0:T(8,128)S(1)} %broadcast_select_fusion.2), channel_id=1, replica_groups=mesh['comp'=2,'gy'=4,'gx'=4] {'comp'}, use_global_device_ids=true, to_apply=%region_6.7 | all-reduce | flops 6240 | bytes 49920 | tf_op jit(solution)/shard_map/psum | solution.py:56
  40.3 13.7 %all-reduce.9.cloned.1.call-done = f32[4,8,8,132]{3,2,1,0:T(8,128)} async-done(((f32[4,8,8,132]{3,2,1,0:T(8,128)}), f32[4,8,8,132]{3,2,1,0:T(8,128)}) %all-reduce.9.cloned.1.call-update) | async-done | bytes 135184 | tf_op jit(solution)/shard_map/psum | solution.py:56
  54.1 5.4 %conditional.8 = (f32[8,8,6,130]{3,2,1,0:T(8,128)S(1)}) conditional(s32[]{:T(128)} %convert_element_type.39, (f32[8,8,8,132]{3,2,1,0:T(8,128)S(1)}, f32[8,8,132]{2,1,0:T(8,128)S(1)}, f32[4,8,8,132]{3,2,1,0:T(8,128)}, f32[8,6,130]{2,1,0:T(8,128)S(1)}) %tuple.55, (f32[8,8,8,132]{3,2,1,0:T(8,128)S(1)}, s32[]{:T(128)}, f32[8,8,132]{2,1,0:T(8,128)S(1)}, ...), branch_computations={%region_7.8_spmd, %region_8.10_spmd} | conditional | flops 2726879 | bytes 9603288 | solution.py:306
  54.1 1.0 %slice_bitcast_fusion.4 = (f32[8,8,132]{2,1,0:T(8,128)S(1)}, f32[8,8,132]{2,1,0:T(8,128)S(1)}, f32[8,8,132]{2,1,0:T(8,128)S(1)}, f32[8,8,132]{2,1,0:T(8,128)S(1)}) fusion(f32[4,8,8,132]{3,2,1,0:T(8,128)} %get-tuple-element.91), kind=kLoop, calls=%fused_computation.84 | loop fusion | bytes 270336 | tf_op jit(solution)/shard_map/cond/branch_0_fun/squeeze | solution.py:259
  55.8 0.8 copy-done
  58.6 0.9 multiply_add_fusion.2
  59.5 0.7 broadcast_select_fusion
  60.5 3.4 %psum.31 = f32[8,4,128]{2,1,0:T(4,128)S(1)} all-reduce(f32[8,4,128]{2,1,0:T(4,128)S(1)} %broadcast_select_fusion.3), channel_id=1, replica_groups=mesh['comp'=2,'gy'=4,'gx'=4] {'comp'}, use_global_device_ids=true, to_apply=%region_16.17 | all-reduce | flops 4096 | bytes 32768 | tf_op jit(solution)/shard_map/psum | solution.py:56
  63.9 15.9 %all-reduce.11.cloned.1.call-done = f32[4,8,6,130]{3,2,1,0:T(8,128)} async-done(((f32[4,8,6,130]{3,2,1,0:T(8,128)}), f32[4,8,6,130]{3,2,1,0:T(8,128)}) %all-reduce.11.cloned.1.call-update) | async-done | bytes 99856 | tf_op jit(solution)/shard_map/psum | solution.py:56
  79.8 4.0 %conditional.11 = (f32[8,8,4,128]{3,2,1,0:T(4,128)S(1)}) conditional(s32[]{:T(128)} %convert_element_type.39, (f32[8,8,6,130]{3,2,1,0:T(8,128)S(1)}, f32[8,6,130]{2,1,0:T(8,128)S(1)}, f32[4,8,6,130]{3,2,1,0:T(8,128)}, f32[8,4,128]{2,1,0:T(4,128)S(1)}) %tuple.61, (f32[8,8,6,130]{3,2,1,0:T(8,128)S(1)}, s32[]{:T(128)}, f32[8,6,130]{2,1,0:T(8,128)S(1)}, ...), branch_computations={%region_17.18_spmd, %region_18.20_spmd} | conditional | flops 1789951 | bytes 5153908 | solution.py:306
  80.0 0.7 copy-done.5
  83.8 0.6 copy-done.6
  (67 shorter events, 8.1 us)
Async XLA Ops:
  6.5 0.7 copy-start.7
  6.5 47.5 %all-reduce.9.cloned.1.call-start = ((), (), s32[]{:S(2)}) async-start(), calls=%async_computation | async-start | bytes 524288 | tf_op jit(solution)/shard_map/psum | solution.py:56
  7.9 8.5 %copy-start.2 = (f32[8,8,4,128]{3,2,1,0:T(4,128)S(1)}, f32[8,8,4,128]{3,2,1,0:T(4,128)}, u32[]{:S(2)}) copy-start(f32[8,8,4,128]{3,2,1,0:T(4,128)} %param.16) | copy-start | bytes 393220
  9.1 6.0 %collective-permute-start = (f32[9,8,2,128]{3,2,1,0:T(2,128)S(1)}, f32[9,8,2,128]{3,2,1,0:T(2,128)S(1)}, u32[]{:S(2)}, u32[]{:S(2)}) collective-permute-start(f32[9,8,2,128]{3,2,1,0:T(2,128)S(1)} %get-tuple-element.212), channel_id=1, source_target_pairs={{0,1},{1,2},{2,3},{3,0},{4,5},{5,6},{6,7},{7,4},{8,9},{9,10},{10,1... | collective-permute-start | bytes 221192 | tf_op jit(solution)/shard_map/ppermute | solution.py:48
  11.2 5.2 %collective-permute-start.1 = (f32[9,8,2,128]{3,2,1,0:T(2,128)S(1)}, f32[9,8,2,128]{3,2,1,0:T(2,128)S(1)}, u32[]{:S(2)}, u32[]{:S(2)}) collective-permute-start(f32[9,8,2,128]{3,2,1,0:T(2,128)S(1)} %get-tuple-element.213), channel_id=1, source_target_pairs={{1,0},{2,1},{3,2},{0,3},{5,4},{6,5},{7,6},{4,7},{9,8},{10,9},{11,1... | collective-permute-start | bytes 221192 | tf_op jit(solution)/shard_map/ppermute | solution.py:49
  16.7 7.7 %collective-permute-start.2 = (f32[9,8,8,2]{3,2,1,0:T(8,128)S(1)}, f32[9,8,8,2]{3,2,1,0:T(8,128)S(1)}, u32[]{:S(2)}, u32[]{:S(2)}) collective-permute-start(f32[9,8,8,2]{3,2,1,0:T(8,128)S(1)} %get-tuple-element.210), channel_id=1, source_target_pairs={{0,4},{4,8},{8,12},{1,5},{5,9},{9,13},{2,6},{6,10},{10,14},{3,7},{... | collective-permute-start | bytes 13832 | tf_op jit(solution)/shard_map/ppermute | solution.py:48
  19.5 13.2 %collective-permute-start.3 = (f32[9,8,8,2]{3,2,1,0:T(8,128)S(1)}, f32[9,8,8,2]{3,2,1,0:T(8,128)S(1)}, u32[]{:S(2)}, u32[]{:S(2)}) collective-permute-start(f32[9,8,8,2]{3,2,1,0:T(8,128)S(1)} %get-tuple-element.211), channel_id=1, source_target_pairs={{4,0},{8,4},{12,8},{5,1},{9,5},{13,9},{6,2},{10,6},{14,10},{7,3},{... | collective-permute-start | bytes 13832 | tf_op jit(solution)/shard_map/ppermute | solution.py:49
  34.3 45.5 %all-reduce.11.cloned.1.call-start = ((), (), s32[]{:S(2)}) async-start(), calls=%async_computation.1 | async-start | bytes 524288 | tf_op jit(solution)/shard_map/psum | solution.py:56
  55.8 0.8 copy-start
  57.4 1.0 %copy-start.1 = (f32[8,8,6,130]{3,2,1,0:T(8,128)S(1)}, f32[8,8,6,130]{3,2,1,0:T(8,128)}, u32[]{:S(2)}) copy-start(f32[8,8,6,130]{3,2,1,0:T(8,128)} %copy-done) | copy-start | bytes 599044 | tf_op jit(solution)/shard_map/cond
  57.5 1.1 %slice-start = ((f32[8,8,6,130]{3,2,1,0:T(8,128)}), f32[8,7,6,130]{3,2,1,0:T(8,128)S(1)}, s32[]{:S(2)}) async-start(f32[8,8,6,130]{3,2,1,0:T(8,128)} %copy-done), calls=%async_computation.2 | async-start | bytes 917504 | tf_op jit(solution)/shard_map/cond/branch_0_fun/slice | solution.py:264
  79.8 0.9 %copy-start.5 = (f32[4,8,6,130]{3,2,1,0:T(8,128)S(1)}, f32[4,8,6,130]{3,2,1,0:T(8,128)}, u32[]{:S(2)}) copy-start(f32[4,8,6,130]{3,2,1,0:T(8,128)} %get-tuple-element.103) | copy-start | bytes 299524 | tf_op jit(solution)/shard_map/cond
  81.1 0.7 copy-start.3
  82.3 0.9 copy-start.4
  82.4 0.9 %slice-start.1 = ((f32[8,8,4,128]{3,2,1,0:T(4,128)}), f32[8,7,4,128]{3,2,1,0:T(4,128)S(1)}, s32[]{:S(2)}) async-start(f32[8,8,4,128]{3,2,1,0:T(4,128)} %copy-done.3), calls=%async_computation.3 | async-start | bytes 229376 | tf_op jit(solution)/shard_map/cond/branch_0_fun/slice | solution.py:264
  83.8 0.7 copy-start.6
Sparse Core Ops, SparseCore 0:
  34.4 19.6 all-reduce.8
  60.4 19.3 all-reduce.10
where the time goes:
time: 91.6 us; the launch traced here: 91.3 us
  waiting for transfers between devices  44.6 us (49%)
  between operations  13.6 us (15%)
  other arithmetic  9.45 us (10%)
  blocking collectives  8.94 us (10%)
  starting transfers between devices  8.39 us (9%)
  local copies, waits for them, and re-layouts  5.99 us (7%)
    psum x2, waiting for transfers between devices, broadcast(): return lax.psum(jnp.where(mine, shard, jnp.zeros_like(shard)), axis)  29.6 us
    ppermute x2, waiting for transfers between devices, extended(): after = lax.ppermute(leading, axis, down)  9.6 us
    psum x2, blocking collectives, broadcast(): return lax.psum(jnp.where(mine, shard, jnp.zeros_like(shard)), axis)  8.94 us
    ppermute x2, waiting for transfers between devices, extended(): before = lax.ppermute(last, axis, up)  5.4 us
    ppermute x2, starting transfers between devices, extended(): before = lax.ppermute(last, axis, up)  4.96 us
    ppermute x2, starting transfers between devices, extended(): after = lax.ppermute(leading, axis, down)  3.38 us
    cond x10, local copies, waits for them, and re-layouts  3.24 us
  transfers between devices with their start and end apart: 6, of which 6 were waited for; matrix products, arithmetic and copies ran while one was open for 1% of the time, Pallas kernels for 0%

commit v1 on v0

--- a/solution.py
+++ b/solution.py
@@ -53,7 +53,7 @@
 
 def broadcast(shard, axis, root):
     mine = lax.axis_index(axis) == root
-    return lax.psum(jnp.where(mine, shard, jnp.zeros_like(shard)), axis)
+    return jnp.sum(lax.all_gather(jnp.where(mine, shard, jnp.zeros_like(shard)), axis), axis=0)
 
 
 def interior(field_in):

time: 91.6 us -> 45.9 us (0.50)
  waiting for transfers between devices: 44.6 us -> 15 us
  between operations: 13.6 us -> 0.2 us
  other arithmetic: 9.45 us -> 5.9 us
  blocking collectives: 8.94 us -> 11.3 us
  local copies, waits for them, and re-layouts: 5.99 us -> 4.6 us
    psum x2 -> x0, waiting for transfers between devices: 29.6 us -> none  [broadcast(): return lax.psum(jnp.where(mine, shard, jnp.zeros_like(shard)), axis)]
    all_gather x0 -> x4, blocking collectives: none -> 11.3 us  [broadcast(): lax.all_gather(jnp.where(mine, shard, jnp.zeros_like(shard)), axis)]
    psum x2 -> x0, blocking collectives: 8.94 us -> none  [broadcast(): return lax.psum(jnp.where(mine, shard, jnp.zeros_like(shard)), axis)]
    cond x10 -> x5, local copies, waits for them, and re-layouts: 3.24 us -> 1.44 us
    select_n x4, other arithmetic: 1.48 us -> 0.05 us  [broadcast(): jnp.where(mine, shard, jnp.zeros_like(shard))]
    concatenate x1, other arithmetic: 1.12 us -> 0.01 us  [local(): padded = extend(jnp.concatenate([current, lit_wet[None]], axis=0), STEPS)]
    squeeze x2 -> x1, local copies, waits for them, and re-layouts: 0.97 us -> 0.02 us  [tracer_update(): flow_full[0]]
    unnamed x6 -> x7, local copies, waits for them, and re-layouts: 0.66 us -> 1.6 us
  transfers between devices with their start and end apart: 6 -> 4, of which waited for: 6 -> 4; matrix products, arithmetic and copies ran while one was open for 1% -> 0% of each run, Pallas kernels for 0% -> 0%
where the time goes in v1:
time: 45.9 us; the launch traced here: 45.7 us
  waiting for transfers between devices  15 us (33%)
  blocking collectives  11.3 us (25%)
  starting transfers between devices  8.34 us (18%)
  other arithmetic  5.9 us (13%)
  local copies, waits for them, and re-layouts  4.6 us (10%)
    all_gather x4, blocking collectives, broadcast(): lax.all_gather(jnp.where(mine, shard, jnp.zeros_like(shard)), axis)  11.3 us
    ppermute x2, waiting for transfers between devices, extended(): after = lax.ppermute(leading, axis, down)  9.6 us
    ppermute x2, waiting for transfers between devices, extended(): before = lax.ppermute(last, axis, up)  5.4 us
    ppermute x2, starting transfers between devices, extended(): before = lax.ppermute(last, axis, up)  4.96 us
    ppermute x2, starting transfers between devices, extended(): after = lax.ppermute(leading, axis, down)  3.38 us
    cond x14, other arithmetic  1.75 us
    unnamed x7, local copies, waits for them, and re-layouts  1.6 us
    cond x4, local copies, waits for them, and re-layouts  1.43 us
  transfers between devices with their start and end apart: 4, of which 4 were waited for; matrix products, arithmetic and copies ran while one was open for 0% of the time, Pallas kernels for 0%

profile of v1, /device:TPU:1, one launch (start us, length us, event | category | flops | bytes accessed | tf_op | source)
XLA Modules:
  0.0 45.7 jit_solution(5904922649295001319)
XLA Ops:
  0.0 0.7 %broadcast_compare_fusion = pred[4,128]{1,0:T(4,128)(4,1)S(1)} fusion(s32[4,128]{1,0:T(4,128)} %param.18), kind=kLoop, calls=%fused_computation.356 | loop fusion | flops 512 | bytes 2560 | tf_op jit(solution)/shard_map/eq | solution.py:311
  0.7 0.9 %copy.7 = f32[8,8,4,128]{3,1,2,0:T(8,128)S(1)} copy(f32[8,8,4,128]{3,2,1,0:T(4,128)} %param.16) | data formatting | bytes 262144 | tf_op args[0]
  1.7 2.2 %collective-permute-start = (f32[9,8,2,128]{3,1,2,0:T(8,128)S(1)}, f32[9,8,2,128]{3,1,2,0:T(8,128)S(1)}, u32[]{:S(2)}, u32[]{:S(2)}) collective-permute-start(f32[9,8,2,128]{3,1,2,0:T(8,128)S(1)} %get-tuple-element.264), channel_id=1, source_target_pairs={{0,1},{1,2},{2,3},{3,0},{4,5},{5,6},{6,7},{7,4},{8,9},{9,10},{10,1... | collective-permute-start | bytes 221192 | tf_op jit(solution)/shard_map/ppermute | solution.py:48
  3.9 2.1 %collective-permute-start.1 = (f32[9,8,2,128]{3,1,2,0:T(8,128)S(1)}, f32[9,8,2,128]{3,1,2,0:T(8,128)S(1)}, u32[]{:S(2)}, u32[]{:S(2)}) collective-permute-start(f32[9,8,2,128]{3,1,2,0:T(8,128)S(1)} %get-tuple-element.265), channel_id=1, source_target_pairs={{1,0},{2,1},{3,2},{0,3},{5,4},{6,5},{7,6},{4,7},{9,8},{10,9},{11,1... | collective-permute-start | bytes 221192 | tf_op jit(solution)/shard_map/ppermute | solution.py:49
  5.9 1.8 %collective-permute-done = f32[9,8,2,128]{3,1,2,0:T(8,128)S(1)} collective-permute-done((f32[9,8,2,128]{3,1,2,0:T(8,128)S(1)}, f32[9,8,2,128]{3,1,2,0:T(8,128)S(1)}, u32[]{:S(2)}, u32[]{:S(2)}) %collective-permute-start) | collective-permute-done | bytes 73760 | tf_op jit(solution)/shard_map/ppermute | solution.py:48
  7.7 1.3 %collective-permute-done.1 = f32[9,8,2,128]{3,1,2,0:T(8,128)S(1)} collective-permute-done((f32[9,8,2,128]{3,1,2,0:T(8,128)S(1)}, f32[9,8,2,128]{3,1,2,0:T(8,128)S(1)}, u32[]{:S(2)}, u32[]{:S(2)}) %collective-permute-start.1) | collective-permute-done | bytes 73760 | tf_op jit(solution)/shard_map/ppermute | solution.py:49
  9.2 2.8 %collective-permute-start.2 = (f32[9,8,8,2]{3,1,2,0:T(8,128)S(1)}, f32[9,8,8,2]{3,1,2,0:T(8,128)S(1)}, u32[]{:S(2)}, u32[]{:S(2)}) collective-permute-start(f32[9,8,8,2]{3,1,2,0:T(8,128)S(1)} %get-tuple-element.262), channel_id=1, source_target_pairs={{0,4},{4,8},{8,12},{1,5},{5,9},{9,13},{2,6},{6,10},{10,14},{3,7},{... | collective-permute-start | bytes 13832 | tf_op jit(solution)/shard_map/ppermute | solution.py:48
  12.0 1.3 %collective-permute-start.3 = (f32[9,8,8,2]{3,1,2,0:T(8,128)S(1)}, f32[9,8,8,2]{3,1,2,0:T(8,128)S(1)}, u32[]{:S(2)}, u32[]{:S(2)}) collective-permute-start(f32[9,8,8,2]{3,1,2,0:T(8,128)S(1)} %get-tuple-element.263), channel_id=1, source_target_pairs={{4,0},{8,4},{12,8},{5,1},{9,5},{13,9},{6,2},{10,6},{14,10},{7,3},{... | collective-permute-start | bytes 13832 | tf_op jit(solution)/shard_map/ppermute | solution.py:49
  13.3 3.6 %collective-permute-done.2 = f32[9,8,8,2]{3,1,2,0:T(8,128)S(1)} collective-permute-done((f32[9,8,8,2]{3,1,2,0:T(8,128)S(1)}, f32[9,8,8,2]{3,1,2,0:T(8,128)S(1)}, u32[]{:S(2)}, u32[]{:S(2)}) %collective-permute-start.2) | collective-permute-done | bytes 4640 | tf_op jit(solution)/shard_map/ppermute | solution.py:48
  17.0 8.3 %collective-permute-done.3 = f32[9,8,8,2]{3,1,2,0:T(8,128)S(1)} collective-permute-done((f32[9,8,8,2]{3,1,2,0:T(8,128)S(1)}, f32[9,8,8,2]{3,1,2,0:T(8,128)S(1)}, u32[]{:S(2)}, u32[]{:S(2)}) %collective-permute-start.3) | collective-permute-done | bytes 4640 | tf_op jit(solution)/shard_map/ppermute | solution.py:49
  25.2 0.3 pad_maximum_fusion.4
  25.7 0.5 %conditional.7 = (f32[8,6,130]{2,1,0:T(8,128)S(1)}, f32[8,6,130]{2,0,1:T(8,128)S(1)}) conditional(s32[]{:T(128)} %convert_element_type.39, (f32[8,8,132]{2,0,1:T(8,128)S(1)}, f32[8,8,8,132]{3,1,2,0:T(8,128)S(1)}) %tuple.53, () %tuple.54), branch_computations={%region_2.4_spmd, %region_4.5_spmd} | conditional | flops 162240 | bytes 1050224 | solution.py:296
  26.2 3.3 %all-gather.1 = f32[16,6,130]{2,0,1:T(8,128)S(1)} all-gather(f32[8,6,130]{2,0,1:T(8,128)S(1)} %broadcast_select_fusion.2), channel_id=3, replica_groups=mesh['comp'=2,'gy'=4,'gx'=4] {'comp'}, dimensions={0}, use_global_device_ids=true | all-gather | bytes 74880 | tf_op jit(solution)/shard_map/all_gather | solution.py:56
  29.6 4.0 %all-gather = f32[8,8,8,132]{3,2,1,0:T(8,128)S(1)} all-gather(f32[4,8,8,132]{3,2,1,0:T(8,128)S(1)} %broadcast_select_fusion), channel_id=2, replica_groups=mesh['comp'=2,'gy'=4,'gx'=4] {'comp'}, dimensions={0}, use_global_device_ids=true | all-gather | bytes 405504 | tf_op jit(solution)/shard_map/all_gather | solution.py:56
  33.6 4.8 %conditional.8 = (f32[8,8,6,130]{3,2,1,0:T(8,128)S(1)}) conditional(s32[]{:T(128)} %convert_element_type.39, (f32[8,8,8,132]{3,1,2,0:T(8,128)S(1)}, f32[8,8,132]{2,0,1:T(8,128)S(1)}, f32[8,8,8,132]{3,2,1,0:T(8,128)S(1)}, f32[8,6,130]{2,1,0:T(8,128)S(1)}) %tuple.55, (f32[8,8,8,132]{3,1,2,0:T(8,128)S(1)}, s32[]{:T(128)}, f32[8,8,132]{2,0,1:T(8,128)S(1)}, ...), branch_computations={%region_5.7_spmd, %region_7.10_spmd} | conditional | flops 2760671 | bytes 10617052 | solution.py:306
  34.7 0.8 %copy-done = f32[8,8,6,130]{3,2,1,0:T(8,128)} copy-done((f32[8,8,6,130]{3,2,1,0:T(8,128)}, f32[8,8,6,130]{3,2,1,0:T(8,128)S(1)}, u32[]{:S(2)}) %copy-start) | copy-done | bytes 199704 | tf_op jit(solution)/shard_map/cond
  36.7 0.6 %copy-done.1 = f32[8,8,6,130]{3,2,1,0:T(8,128)S(1)} copy-done((f32[8,8,6,130]{3,2,1,0:T(8,128)S(1)}, f32[8,8,6,130]{3,2,1,0:T(8,128)}, u32[]{:S(2)}) %copy-start.1) | copy-done | bytes 199704 | tf_op jit(solution)/shard_map/cond
  37.5 0.9 %multiply_add_fusion = f32[8,8,6,130]{3,2,1,0:T(8,128)S(1)} fusion(f32[8,8,6,130]{3,2,1,0:T(8,128)S(1)} %bitcast_dynamic-update-slice_fusion, f32[8,8,6,130]{3,2,1,0:T(8,128)S(1)} %copy-done.1, f32[8,7,6,130]{3,2,1,0:T(8,128)S(1)} %slice-done, f32[8,8,8,132]{3,2,1,0:T(8,128)S(1)} %copy.13, f32[8,6,130]{2,1,0:T(8,128)S(1)} %get-tuple-element.191, ...), kind=kLoop, calls=%fused_computation.26 | loop fusion | flops 1896960 | bytes 2021760 | tf_op jit(solution)/shard_map/cond/branch_0_fun/add | solution.py:267
  38.5 0.2 conditional.10
  38.8 1.8 %all-gather.3 = f32[16,4,128]{2,1,0:T(4,128)S(1)} all-gather(f32[8,4,128]{2,1,0:T(4,128)S(1)} %broadcast_select_fusion.3), channel_id=5, replica_groups=mesh['comp'=2,'gy'=4,'gx'=4] {'comp'}, dimensions={0}, use_global_device_ids=true | all-gather | bytes 49152 | tf_op jit(solution)/shard_map/all_gather | solution.py:56
  40.7 2.1 %all-gather.2 = f32[8,8,6,130]{3,1,2,0:T(8,128)S(1)} all-gather(f32[4,8,6,130]{3,1,2,0:T(8,128)S(1)} %broadcast_select_fusion.1), channel_id=4, replica_groups=mesh['comp'=2,'gy'=4,'gx'=4] {'comp'}, dimensions={0}, use_global_device_ids=true | all-gather | bytes 299520 | tf_op jit(solution)/shard_map/all_gather | solution.py:56
  42.8 2.3 %conditional.11 = (f32[8,8,4,128]{3,2,1,0:T(4,128)S(1)}) conditional(s32[]{:T(128)} %convert_element_type.39, (f32[8,8,6,130]{3,2,1,0:T(8,128)S(1)}, f32[8,6,130]{2,0,1:T(8,128)S(1)}, f32[8,8,6,130]{3,1,2,0:T(8,128)S(1)}, f32[8,4,128]{2,1,0:T(4,128)S(1)}) %tuple.61, (f32[8,8,6,130]{3,2,1,0:T(8,128)S(1)}, s32[]{:T(128)}, ...), branch_computations={%region_15.17_spmd, %region_17.20_spmd} | conditional | flops 1814911 | bytes 4140300 | solution.py:306
  44.5 0.5 %multiply_add_fusion.5 = f32[8,8,4,128]{3,2,1,0:T(4,128)S(1)} fusion(f32[8,8,4,128]{3,2,1,0:T(4,128)S(1)} %constant_dynamic-update-slice_fusion, f32[8,8,4,128]{3,2,1,0:T(4,128)S(1)} %subtract_multiply_fusion.1, f32[8,7,4,128]{3,2,1,0:T(4,128)S(1)} %slice.798, f32[8,8,6,130]{3,2,1,0:T(8,128)S(1)} %get-tuple-element.113, ...), kind=kLoop, calls=%fused_computation.211 | loop fusion | flops 1245184 | bytes 1327104 | tf_op jit(solution)/shard_map/cond/branch_0_fun/add | solution.py:267
  45.0 0.6 %copy-done.3 = f32[8,8,4,128]{3,2,1,0:T(4,128)} copy-done((f32[8,8,4,128]{3,2,1,0:T(4,128)}, f32[8,8,4,128]{3,2,1,0:T(4,128)S(1)}, u32[]{:S(2)}) %copy-start.3) | copy-done | bytes 131096
  (69 shorter events, 5.2 us)
Async XLA Ops:
  0.7 0.9 %copy-start.4 = (f32[4,128]{1,0:T(4,128)S(1)}, f32[4,128]{1,0:T(4,128)}, u32[]{:S(2)}) copy-start(f32[4,128]{1,0:T(4,128)} %param.17) | copy-start | bytes 6148
  0.7 1.0 %copy-start.5 = (s32[4,128]{1,0:T(4,128)S(1)}, s32[4,128]{1,0:T(4,128)}, u32[]{:S(2)}) copy-start(s32[4,128]{1,0:T(4,128)} %param.19) | copy-start | bytes 6148
  1.7 6.0 %collective-permute-start = (f32[9,8,2,128]{3,1,2,0:T(8,128)S(1)}, f32[9,8,2,128]{3,1,2,0:T(8,128)S(1)}, u32[]{:S(2)}, u32[]{:S(2)}) collective-permute-start(f32[9,8,2,128]{3,1,2,0:T(8,128)S(1)} %get-tuple-element.264), channel_id=1, source_target_pairs={{0,1},{1,2},{2,3},{3,0},{4,5},{5,6},{6,7},{7,4},{8,9},{9,10},{10,1... | collective-permute-start | bytes 221192 | tf_op jit(solution)/shard_map/ppermute | solution.py:48
  3.9 5.2 %collective-permute-start.1 = (f32[9,8,2,128]{3,1,2,0:T(8,128)S(1)}, f32[9,8,2,128]{3,1,2,0:T(8,128)S(1)}, u32[]{:S(2)}, u32[]{:S(2)}) collective-permute-start(f32[9,8,2,128]{3,1,2,0:T(8,128)S(1)} %get-tuple-element.265), channel_id=1, source_target_pairs={{1,0},{2,1},{3,2},{0,3},{5,4},{6,5},{7,6},{4,7},{9,8},{10,9},{11,1... | collective-permute-start | bytes 221192 | tf_op jit(solution)/shard_map/ppermute | solution.py:49
  9.2 7.7 %collective-permute-start.2 = (f32[9,8,8,2]{3,1,2,0:T(8,128)S(1)}, f32[9,8,8,2]{3,1,2,0:T(8,128)S(1)}, u32[]{:S(2)}, u32[]{:S(2)}) collective-permute-start(f32[9,8,8,2]{3,1,2,0:T(8,128)S(1)} %get-tuple-element.262), channel_id=1, source_target_pairs={{0,4},{4,8},{8,12},{1,5},{5,9},{9,13},{2,6},{6,10},{10,14},{3,7},{... | collective-permute-start | bytes 13832 | tf_op jit(solution)/shard_map/ppermute | solution.py:48
  12.0 13.2 %collective-permute-start.3 = (f32[9,8,8,2]{3,1,2,0:T(8,128)S(1)}, f32[9,8,8,2]{3,1,2,0:T(8,128)S(1)}, u32[]{:S(2)}, u32[]{:S(2)}) collective-permute-start(f32[9,8,8,2]{3,1,2,0:T(8,128)S(1)} %get-tuple-element.263), channel_id=1, source_target_pairs={{4,0},{8,4},{12,8},{5,1},{9,5},{13,9},{6,2},{10,6},{14,10},{7,3},{... | collective-permute-start | bytes 13832 | tf_op jit(solution)/shard_map/ppermute | solution.py:49
  34.7 0.8 %copy-start = (f32[8,8,6,130]{3,2,1,0:T(8,128)}, f32[8,8,6,130]{3,2,1,0:T(8,128)S(1)}, u32[]{:S(2)}) copy-start(f32[8,8,6,130]{3,2,1,0:T(8,128)S(1)} %subtract_multiply_fusion) | copy-start | bytes 599044 | tf_op jit(solution)/shard_map/cond
  36.3 1.0 %copy-start.1 = (f32[8,8,6,130]{3,2,1,0:T(8,128)S(1)}, f32[8,8,6,130]{3,2,1,0:T(8,128)}, u32[]{:S(2)}) copy-start(f32[8,8,6,130]{3,2,1,0:T(8,128)} %copy-done) | copy-start | bytes 599044 | tf_op jit(solution)/shard_map/cond
  36.4 1.1 %slice-start = ((f32[8,8,6,130]{3,2,1,0:T(8,128)}), f32[8,7,6,130]{3,2,1,0:T(8,128)S(1)}, s32[]{:S(2)}) async-start(f32[8,8,6,130]{3,2,1,0:T(8,128)} %copy-done), calls=%async_computation | async-start | bytes 917504 | tf_op jit(solution)/shard_map/cond/branch_0_fun/slice | solution.py:264
  45.0 0.7 %copy-start.3 = (f32[8,8,4,128]{3,2,1,0:T(4,128)}, f32[8,8,4,128]{3,2,1,0:T(4,128)S(1)}, u32[]{:S(2)}) copy-start(f32[8,8,4,128]{3,2,1,0:T(4,128)S(1)} %get-tuple-element.286) | copy-start | bytes 393220
